TPU v7x, 32 devices: a whole 2x2x4 slice. The times are simulated.
32 devices in a mesh: groups: 2 (over x), seq: 16 (over z, y, core).
Axes of the slice: x: 2, y: 2, z: 4, core: 2. Of those that a mesh axis runs over, the one named last changes fastest.
Arguments:
- query_seq: bfloat16 [8192, 6144], P(('groups', 'seq')), parts along dimension 0, may hold values from -15 to 15
- key_seq: bfloat16 [8192, 6144], P(('groups', 'seq')), parts along dimension 0, may hold values from -15 to 15
- value_seq: bfloat16 [8192, 6144], P(('groups', 'seq')), parts along dimension 0, may hold values from -288 to 288
- conv_kernel: bfloat16 [3, 4, 6144], replicated, may hold values from -3 to 3
- feature_map: bfloat16 [128, 128], replicated, may hold values from -1.5 to 1.5
- norm_gain: float32 [6144], replicated, may hold values from 0.25 to 1.75
Outputs:
- attended: bfloat16 [8192, 6144], P(('groups', 'seq')), parts along dimension 0
There are 2 independent parts, one for each index of `groups`. A program takes and returns all parts, laid end to end along the dimension named above; an argument that names none is the same for every part. Nothing has to cross between parts.
All inputs are finite; a program needn't handle non-finite values.
Results may differ from a plain program's by a relative error of at most 0.012.
The roundings to bfloat16 on the way count: a program that leaves them out, or rounds other values in their place, can miss the bound.
Values may be sent and summed in bfloat16 or wider, within the bound.
A program may use at most 128 MiB of HBM per device.

v0:
```python
import functools

import jax
import jax.numpy as jnp
from jax import lax
from jax.experimental import pallas as pl
from jax.experimental.pallas import tpu as pltpu
from jax.sharding import PartitionSpec as P

MESH = pl.DeviceIdType.MESH
F32 = jnp.float32
BF16 = jnp.bfloat16
RIM = 8
ROWS = 64
Z_LAG = 2
Y_LAG = 3
P_LAG = 2
Q_FIRST = 12
Q_SLOPE = 3


def short_conv(buf, rim, taps, which, col, width):
    tap_rows = taps[which, :, pl.ds(col, width)].astype(F32)
    tap_count = tap_rows.shape[0]
    length = buf.shape[0]
    above = rim[:, pl.ds(col, width)].astype(F32)
    out = []
    for start in range(0, length, ROWS):
        rows = buf[start : start + ROWS, pl.ds(col, width)].astype(F32)
        padded = jnp.concatenate([above, rows], axis=0)
        total = tap_rows[0:1] * rows
        for offset in range(1, tap_count):
            window = padded[RIM - offset : RIM - offset + ROWS]
            total = total + tap_rows[offset : offset + 1] * window
        out.append(total.astype(BF16))
        above = rows[ROWS - RIM :]
    return jnp.concatenate(out, axis=0)


def features(conv_rows, wide_map):
    projected = jnp.dot(conv_rows, wide_map[...], preferred_element_type=F32)
    return jnp.where(projected > 0, projected + 1.0, jnp.exp(projected)).astype(BF16)


def kernel(
    devices,
    q_hbm,
    k_hbm,
    v_hbm,
    taps,
    feature_map,
    gain,
    out_buf,
    q_buf,
    k_buf,
    v_buf,
    q_rim,
    k_rim,
    v_rim,
    wide_map,
    q_feat,
    k_feat,
    v_conv,
    mixed,
    own_state,
    x_out,
    x_in,
    z_out,
    z_in,
    y_out,
    y_in,
    p_out,
    prefix,
    load_sem,
    rim_sem,
    x_sem,
    z_sem,
    y_sem,
    p_sem,
):
    tokens, width = q_buf.shape
    dim = feature_map.shape[0]
    pair = 2 * dim
    chunk = 2 * pair
    chunks = width // chunk
    me = lax.axis_index("seq")
    core = lax.rem(me, 2)
    y = lax.rem(me // 2, 2)
    z = me // 4
    planes = devices // 4
    partner = me + 1 - 2 * core
    across = me + 2 - 4 * y

    def load(hbm, buf, which, c):
        cols = pl.ds(pl.multiple_of(c * chunk, chunk), chunk)
        return pltpu.make_async_copy(hbm.at[:, cols], buf.at[:, cols], load_sem.at[which, c])

    @pl.loop(0, chunks)
    def _(c):
        load(k_hbm, k_buf, 1, c).start()
        load(v_hbm, v_buf, 2, c).start()

    barrier = pltpu.get_barrier_semaphore()

    def greet(target):
        pl.semaphore_signal(barrier, inc=1, device_id={"seq": target}, device_id_type=MESH)

    greet(partner)
    greet(across)

    @pl.when(me > 0)
    def _():
        greet(me - 1)

    @pl.when(me < devices - 1)
    def _():
        greet(me + 1)

    @pl.when(z > 0)
    def _():
        greet(me - 4)

    @pl.when(z < planes - 1)
    def _():
        greet(me + 4)

    @pl.loop(0, chunks)
    def _(c):
        load(q_hbm, q_buf, 0, c).start()

    wide_map[...] = jnp.zeros_like(wide_map)
    wide_map[:dim, :dim] = feature_map[...]
    wide_map[dim:, dim:] = feature_map[...]

    @pl.when(me == 0)
    def _():
        q_rim[...] = jnp.zeros_like(q_rim)
        k_rim[...] = jnp.zeros_like(k_rim)
        v_rim[...] = jnp.zeros_like(v_rim)

    @pl.when(z == 0)
    def _():
        @pl.loop(0, chunks)
        def _(c):
            z_in[c] = jnp.zeros(z_in.shape[1:], BF16)

    edges = [(me > 0), (me < devices - 1), (z > 0), (z < planes - 1)]
    pl.semaphore_wait(barrier, 2 + sum(e.astype(jnp.int32) for e in edges))

    def rim_copy(which, c):
        hbm, rim = ((q_hbm, q_rim), (k_hbm, k_rim), (v_hbm, v_rim))[which]
        cols = pl.ds(pl.multiple_of(c * chunk, chunk), chunk)
        return pltpu.make_async_remote_copy(
            src_ref=hbm.at[pl.ds(tokens - RIM, RIM), cols],
            dst_ref=rim.at[:, cols],
            send_sem=rim_sem.at[0, which, c],
            recv_sem=rim_sem.at[1, which, c],
            device_id={"seq": lax.rem(me + 1, devices)},
            device_id_type=MESH,
        )

    @pl.when(me < devices - 1)
    def _():
        @pl.loop(0, chunks)
        def _(c):
            rim_copy(1, c).start()
            rim_copy(2, c).start()

        @pl.loop(0, chunks)
        def _(c):
            rim_copy(0, c).start()

    def send(src, dst, sem, c, h, target):
        rows = pl.ds(h * dim, dim)
        return pltpu.make_async_remote_copy(
            src_ref=src.at[rows],
            dst_ref=dst.at[rows],
            send_sem=sem.at[0, c, h],
            recv_sem=sem.at[1, c, h],
            device_id={"seq": target},
            device_id_type=MESH,
        )

    def x_copy(c, h):
        return send(x_out.at[c], x_in.at[c], x_sem, c, h, partner)

    def z_copy(c, h):
        return send(z_out.at[c], z_in.at[c], z_sem, c, h, lax.rem(me + 4, devices))

    def y_copy(c, h):
        return send(y_out.at[c], y_in.at[c], y_sem, c, h, across)

    def p_copy(c, h):
        return send(p_out.at[c], prefix.at[c, core], p_sem, c, h, partner)

    def pair_state(col):
        k_rows = short_conv(k_buf, k_rim, taps, 1, col, pair)
        v_rows = short_conv(v_buf, v_rim, taps, 2, col, pair)
        feat = features(k_rows, wide_map)
        k_feat[:, pl.ds(col, pair)] = feat
        v_conv[:, pl.ds(col, pair)] = v_rows
        both = lax.dot_general(feat, v_rows, (((0,), (0,)), ((), ())), preferred_element_type=F32)
        return both[:dim, :dim], both[dim:, dim:]

    def states(c):
        load(k_hbm, k_buf, 1, c).wait()
        load(v_hbm, v_buf, 2, c).wait()

        @pl.when(me > 0)
        def _():
            rim_copy(1, c).wait_recv()
            rim_copy(2, c).wait_recv()

        for mine in (False, True):
            side = core if mine else 1 - core
            col = pl.multiple_of(c * chunk + side * pair, pair)
            first, second = pair_state(col)
            if mine:
                own_state[c, :dim] = first
                own_state[c, dim:] = second
            else:
                x_out[c, :dim] = first.astype(BF16)
                x_out[c, dim:] = second.astype(BF16)

        x_copy(c, 0).start()
        x_copy(c, 1).start()

    def relay_z(c):
        for h in range(2):
            rows = pl.ds(h * dim, dim)
            x_copy(c, h).wait_recv()

            @pl.when(z > 0)
            def _():
                z_copy(c, h).wait_recv()

            before = z_in[c, rows].astype(F32)
            chip = own_state[c, rows] + x_in[c, rows].astype(F32)
            z_out[c, rows] = (before + chip).astype(BF16)

            @pl.when(z < planes - 1)
            def _():
                z_copy(c, h).start()

            y_out[c, rows] = (before + jnp.where(y == 0, chip, 0.0)).astype(BF16)
            y_copy(c, h).start()

    def relay_y(c):
        for h in range(2):
            rows = pl.ds(h * dim, dim)
            y_copy(c, h).wait_recv()
            earlier = z_in[c, rows].astype(F32) + y_in[c, rows].astype(F32)
            p_out[c, rows] = (earlier + jnp.where(core == 0, own_state[c, rows], 0.0)).astype(BF16)
            p_copy(c, h).start()
            own = earlier + jnp.where(core == 1, x_in[c, rows].astype(F32), 0.0)
            prefix[c, core, rows] = own.astype(BF16)

    def local_mix(c):
        load(q_hbm, q_buf, 0, c).wait()

        @pl.when(me > 0)
        def _():
            rim_copy(0, c).wait_recv()

        row = lax.broadcasted_iota(jnp.int32, (tokens, tokens), 0)
        causal = row >= lax.broadcasted_iota(jnp.int32, (tokens, tokens), 1)
        for side in range(2):
            col = pl.multiple_of(c * chunk + side * pair, pair)
            q_rows = short_conv(q_buf, q_rim, taps, 0, col, pair)
            feat = features(q_rows, wide_map)
            q_feat[:, pl.ds(col, pair)] = feat
            for head in range(2):
                cols = pl.ds(pl.multiple_of(col + head * dim, dim), dim)
                scores = lax.dot_general(
                    feat[:, head * dim : (head + 1) * dim],
                    k_feat[:, cols],
                    (((1,), (1,)), ((), ())),
                    preferred_element_type=F32,
                )
                weights = jnp.where(causal, scores, 0.0).astype(BF16)
                mixed[:, cols] = jnp.dot(weights, v_conv[:, cols], preferred_element_type=F32)

    def finish(c):
        p_copy(c, 0).wait_recv()
        p_copy(c, 1).wait_recv()
        for head in range(4):
            cols = pl.ds(pl.multiple_of(c * chunk + head * dim, dim), dim)
            state = prefix[c, head // 2, (head % 2) * dim : (head % 2 + 1) * dim]
            rows = mixed[:, cols] + jnp.dot(q_feat[:, cols], state, preferred_element_type=F32)
            scale = lax.rsqrt(jnp.mean(rows * rows, axis=-1, keepdims=True) + 1e-06)
            out_buf[:, cols] = (rows * scale * gain[:, cols]).astype(BF16)

    z_lag = 1 + Z_LAG * z
    y_lag = z_lag + Y_LAG
    q_lag = jnp.maximum(Q_FIRST - Q_SLOPE * z, 1)
    last_lag = jnp.maximum(y_lag + P_LAG, q_lag)

    def at(step, lag, work):
        c = step - lag

        @pl.when((c >= 0) & (c < chunks))
        def _():
            work(c)

    @pl.loop(0, chunks + last_lag)
    def _(step):
        at(step, 0, states)
        at(step, z_lag, relay_z)
        at(step, q_lag, local_mix)
        at(step, y_lag, relay_y)
        at(step, last_lag, finish)

    @pl.when(me < devices - 1)
    def _():
        @pl.loop(0, chunks)
        def _(c):
            for which in range(3):
                rim_copy(which, c).wait_send()

    @pl.loop(0, chunks)
    def _(c):
        for h in range(2):
            x_copy(c, h).wait_send()
            y_copy(c, h).wait_send()
            p_copy(c, h).wait_send()

    @pl.when(z < planes - 1)
    def _():
        @pl.loop(0, chunks)
        def _(c):
            for h in range(2):
                z_copy(c, h).wait_send()


def on_device(query_seq, key_seq, value_seq, conv_kernel, feature_map, norm_gain):
    tokens, width = query_seq.shape
    dim = feature_map.shape[0]
    devices = lax.axis_size("seq")
    chunks = width // (4 * dim)
    rows = pltpu.VMEM((tokens, width), BF16)
    rim = pltpu.VMEM((RIM, width), BF16)
    slots = pltpu.VMEM((chunks, 2 * dim, dim), BF16)
    ways = pltpu.SemaphoreType.DMA((2, chunks, 2))
    hbm = pl.BlockSpec(memory_space=pl.ANY)
    vmem = pl.BlockSpec(memory_space=pltpu.VMEM)
    return pl.pallas_call(
        functools.partial(kernel, devices),
        out_shape=pltpu.MemorySpace.VMEM((tokens, width), BF16),
        in_specs=[hbm, hbm, hbm, vmem, vmem, vmem],
        out_specs=vmem,
        scratch_shapes=[
            rows,
            rows,
            rows,
            rim,
            rim,
            rim,
            pltpu.VMEM((2 * dim, 2 * dim), BF16),
            rows,
            rows,
            rows,
            pltpu.VMEM((tokens, width), F32),
            pltpu.VMEM((chunks, 2 * dim, dim), F32),
            slots,
            slots,
            slots,
            slots,
            slots,
            slots,
            slots,
            pltpu.VMEM((chunks, 2, 2 * dim, dim), BF16),
            pltpu.SemaphoreType.DMA((3, chunks)),
            pltpu.SemaphoreType.DMA((2, 3, chunks)),
            ways,
            ways,
            ways,
            ways,
        ],
        compiler_params=pltpu.CompilerParams(
            collective_id=0, has_side_effects=True, vmem_limit_bytes=60 * 1024 * 1024
        ),
        name="layer",
    )(query_seq, key_seq, value_seq, conv_kernel, feature_map, norm_gain.reshape(1, width))


def solution(mesh):
    split = P(("groups", "seq"), None)
    return jax.shard_map(
        on_device,
        mesh=mesh,
        in_specs=(split, split, split, P(), P(), P()),
        out_specs=split,
        check_vma=False,
    )
```

profile of v0, /device:TPU:25, one launch (start us, length us, event | category | flops | bytes accessed | tf_op | source)
XLA Modules:
  0.0 42.5 jit_solution(3488612260619939279)
XLA Ops:
  0.0 40.8 %layer.1 = bf16[256,6144]{1,0:T(8,128)(2,1)S(1)} custom-call(bf16[256,6144]{1,0:T(8,128)(2,1)} %q_hbm.1, bf16[256,6144]{1,0:T(8,128)(2,1)} %k_hbm.1, bf16[256,6144]{1,0:T(8,128)(2,1)} %v_hbm.1, bf16[3,4,6144]{2,1,0:T(4,128)(2,1)} %taps.1, bf16[128,128]{1,0:T(8,128)(2,1)} %feature_map.1, f32[1,6144]{1,0:T(1,128)} %bitcast.1), custom_call_target="tpu_custom_call" | custom-call | tf_op jit(solution)/shard_map/layer/pallas_call | solution.py:346
  40.8 1.7 %copy.8 = bf16[256,6144]{1,0:T(8,128)(2,1)} copy(bf16[256,6144]{1,0:T(8,128)(2,1)S(1)} %layer.1) | data formatting | bytes 6291456
where the time goes:
time: 42.9 us; the launch traced here: 42.5 us
  Pallas kernels  40.8 us (95%)
  local copies, waits for them, and re-layouts  1.67 us (4%)
    pallas_call x1, Pallas kernels, on_device(): pl.pallas_call(functools.partial(kernel, devices), out_shape=pltpu.Memory...  40.8 us
    unnamed x1, local copies, waits for them, and re-layouts  1.67 us

commit v1 on v0

v1 whole, which is shorter than its diff:
```python
import functools

import jax
import jax.numpy as jnp
from jax import lax
from jax.experimental import pallas as pl
from jax.experimental.pallas import tpu as pltpu
from jax.sharding import PartitionSpec as P

MESH = pl.DeviceIdType.MESH
F32 = jnp.float32
BF16 = jnp.bfloat16
RIM = 8
HALO = 4
LANES = 128
X_LAG = 2
Y_LAG = 4
Z_LAG = 4
R_LAG = 4
P_LAG = 2
MIX_LAG = 12


def short_conv(buf, halo, taps, which, col, width, wide):
    tap_count = taps.shape[1]
    length = buf.shape[0]
    out = []
    for j in range(width // LANES):
        lanes = pl.ds(pl.multiple_of(col + j * LANES, LANES), LANES)
        tall = wide.at[j]
        tap_rows = taps[which, :, lanes].astype(F32)
        tall[RIM - HALO : RIM] = halo[which, :, lanes].astype(F32)
        rows = buf[:, lanes].astype(F32)
        tall[RIM:] = rows
        total = tap_rows[0:1] * rows
        for offset in range(1, tap_count):
            total = total + tap_rows[offset : offset + 1] * tall[RIM - offset : RIM - offset + length]
        out.append(total.astype(BF16))
    return jnp.concatenate(out, axis=1)


def features(conv_rows, wide_map):
    projected = jnp.dot(conv_rows, wide_map[...], preferred_element_type=F32)
    return jnp.where(projected > 0, projected + 1.0, jnp.exp(projected)).astype(BF16)


def kernel(
    devices,
    q_hbm,
    k_hbm,
    v_hbm,
    taps,
    feature_map,
    gain,
    out_buf,
    q_buf,
    k_buf,
    v_buf,
    tail,
    halo_out,
    halo,
    wide,
    wide_map,
    q_feat,
    k_feat,
    v_conv,
    mixed,
    own_state,
    x_out,
    x_in,
    raw_out,
    raw_in,
    z_out,
    z_in,
    res_out,
    res_in,
    p_out,
    prefix,
    load_sem,
    tail_sem,
    send_sem,
    halo_sem,
    x_sem,
    raw_sem,
    z_sem,
    res_sem,
    p_sem,
):
    tokens, width = q_buf.shape
    half = tokens // 2
    dim = feature_map.shape[0]
    pair = 2 * dim
    chunk = 2 * pair
    chunks = width // chunk
    pieces = halo_sem.shape[1]
    per_piece = chunks // pieces
    me = lax.axis_index("seq")
    core = lax.rem(me, 2)
    y = lax.rem(me // 2, 2)
    z = me // 4
    planes = devices // 4
    partner = me + 1 - 2 * core
    across = me + 2 - 4 * y
    sources = (q_hbm, k_hbm, v_hbm)

    def load_tail(which):
        rows = pl.ds(tokens - RIM, RIM)
        return pltpu.make_async_copy(sources[which].at[rows], tail.at[which], tail_sem.at[which])

    def load(buf, which, c):
        cols = pl.ds(pl.multiple_of(c * chunk, chunk), chunk)
        return pltpu.make_async_copy(sources[which].at[:, cols], buf.at[:, cols], load_sem.at[which, c])

    for which in (1, 2, 0):
        load_tail(which).start()

    @pl.loop(0, chunks)
    def _(c):
        load(k_buf, 1, c).start()
        load(v_buf, 2, c).start()

    barrier = pltpu.get_barrier_semaphore()

    def greet(target):
        pl.semaphore_signal(barrier, inc=1, device_id={"seq": target}, device_id_type=MESH)

    greet(partner)
    greet(across)

    @pl.when(me > 0)
    def _():
        greet(me - 1)

    @pl.when(me < devices - 1)
    def _():
        greet(me + 1)

    @pl.when(z > 0)
    def _():
        greet(me - 4)

    @pl.when(z < planes - 1)
    def _():
        greet(me + 4)

    @pl.loop(0, chunks)
    def _(c):
        load(q_buf, 0, c).start()

    wide_map[...] = jnp.zeros_like(wide_map)
    wide_map[:dim, :dim] = feature_map[...]
    wide_map[dim:, dim:] = feature_map[...]

    @pl.when(me == 0)
    def _():
        halo[...] = jnp.zeros_like(halo)

    @pl.when(z == 0)
    def _():
        @pl.loop(0, chunks)
        def _(c):
            z_in[c] = jnp.zeros(z_in.shape[1:], BF16)

    for which in (1, 2, 0):
        load_tail(which).wait()
        halo_out[which] = tail[which].astype(F32)[RIM - HALO :].astype(BF16)

    edges = [(me > 0), (me < devices - 1), (z > 0), (z < planes - 1)]
    pl.semaphore_wait(barrier, 2 + sum(e.astype(jnp.int32) for e in edges))

    def remote(src, dst, kind, recv_sem, target):
        return pltpu.make_async_remote_copy(
            src_ref=src,
            dst_ref=dst,
            send_sem=send_sem.at[kind],
            recv_sem=recv_sem,
            device_id={"seq": target},
            device_id_type=MESH,
        )

    def halo_copy(which, piece):
        size = width // pieces
        cols = pl.ds(pl.multiple_of(piece * size, size), size)
        return remote(
            halo_out.at[which, :, cols],
            halo.at[which, :, cols],
            0,
            halo_sem.at[which, piece],
            lax.rem(me + 1, devices),
        )

    @pl.when(me < devices - 1)
    def _():
        @pl.loop(0, pieces)
        def _(piece):
            halo_copy(1, piece).start()
            halo_copy(2, piece).start()

        @pl.loop(0, pieces)
        def _(piece):
            halo_copy(0, piece).start()

    def wait_halo(c, which):
        @pl.when((me > 0) & (lax.rem(c, per_piece) == 0))
        def _():
            for w in which:
                halo_copy(w, c // per_piece).wait_recv()

    lead = pl.ds(pl.multiple_of(y * dim, dim), dim)
    other = pl.ds(pl.multiple_of((1 - y) * dim, dim), dim)

    def x_copy(c):
        return remote(x_out.at[c], x_in.at[c], 1, x_sem.at[c], partner)

    def raw_copy(c):
        return remote(raw_out.at[c], raw_in.at[c], 2, raw_sem.at[c], across)

    def z_copy(c):
        return remote(z_out.at[c], z_in.at[c], 3, z_sem.at[c], lax.rem(me + 4, devices))

    def res_copy(c):
        return remote(res_out.at[c], res_in.at[c], 4, res_sem.at[c], across)

    def p_copy(c, h):
        rows = pl.ds(pl.multiple_of(h * dim, dim), dim)
        return remote(p_out.at[c, rows], prefix.at[c, core, rows], 5, p_sem.at[c, h], partner)

    def states(c):
        load(k_buf, 1, c).wait()
        load(v_buf, 2, c).wait()
        wait_halo(c, (1, 2))
        found = []
        for side in range(2):
            turn = 1 - core if side == 0 else core
            col = pl.multiple_of(c * chunk + turn * pair, pair)
            k_rows = short_conv(k_buf, halo, taps, 1, col, pair, wide.at[2 * side])
            v_rows = short_conv(v_buf, halo, taps, 2, col, pair, wide.at[2 * side + 1])
            feat = features(k_rows, wide_map)
            k_feat[:, pl.ds(col, pair)] = feat
            v_conv[:, pl.ds(col, pair)] = v_rows
            both = lax.dot_general(feat, v_rows, (((0,), (0,)), ((), ())), preferred_element_type=F32)
            found.append((both[:dim, :dim], both[dim:, dim:]))
        x_out[c, :dim] = found[0][0].astype(BF16)
        x_out[c, dim:] = found[0][1].astype(BF16)
        own_state[c, :dim] = found[1][0]
        own_state[c, dim:] = found[1][1]
        x_copy(c).start()

    def relay_raw(c):
        x_copy(c).wait_recv()
        raw_out[c] = (own_state[c, other] + x_in[c, other].astype(F32)).astype(BF16)
        raw_copy(c).start()

    def hand_on(c, h, rows, earlier):
        p_out[c, rows] = (earlier + jnp.where(core == 0, own_state[c, rows], 0.0)).astype(BF16)
        p_copy(c, h).start()
        own = earlier + jnp.where(core == 1, x_in[c, rows].astype(F32), 0.0)
        prefix[c, core, rows] = own.astype(BF16)

    def relay_z(c):
        raw_copy(c).wait_recv()

        @pl.when(z > 0)
        def _():
            z_copy(c).wait_recv()

        before = z_in[c].astype(F32)
        chip = own_state[c, lead] + x_in[c, lead].astype(F32)
        far = raw_in[c].astype(F32)
        z_out[c] = (before + chip + far).astype(BF16)

        @pl.when(z < planes - 1)
        def _():
            z_copy(c).start()

        res_out[c] = (before + jnp.where(y == 0, chip, 0.0)).astype(BF16)
        res_copy(c).start()
        hand_on(c, y, lead, before + jnp.where(y == 1, far, 0.0))

    def relay_res(c):
        res_copy(c).wait_recv()
        hand_on(c, 1 - y, other, res_in[c].astype(F32))

    def local_mix(c):
        load(q_buf, 0, c).wait()
        wait_halo(c, (0,))
        row = lax.broadcasted_iota(jnp.int32, (half, half), 0)
        causal = row >= lax.broadcasted_iota(jnp.int32, (half, half), 1)
        for side in range(2):
            col = pl.multiple_of(c * chunk + side * pair, pair)
            q_rows = short_conv(q_buf, halo, taps, 0, col, pair, wide.at[side])
            feat = features(q_rows, wide_map)
            q_feat[:, pl.ds(col, pair)] = feat
            for head in range(2):
                cols = pl.ds(pl.multiple_of(col + head * dim, dim), dim)
                scores = lax.dot_general(
                    feat[:, head * dim : (head + 1) * dim],
                    k_feat[:, cols],
                    (((1,), (1,)), ((), ())),
                    preferred_element_type=F32,
                )
                upper = jnp.where(causal, scores[:half, :half], 0.0).astype(BF16)
                left = scores[half:, :half].astype(BF16)
                lower = jnp.where(causal, scores[half:, half:], 0.0).astype(BF16)
                values = v_conv[:, cols]
                mixed[:half, cols] = jnp.dot(upper, values[:half], preferred_element_type=F32)
                mixed[half:, cols] = jnp.dot(
                    jnp.concatenate([left, lower], axis=1), values, preferred_element_type=F32
                )

    def finish(c):
        p_copy(c, 0).wait_recv()
        p_copy(c, 1).wait_recv()
        for head in range(4):
            cols = pl.ds(pl.multiple_of(c * chunk + head * dim, dim), dim)
            state = prefix[c, head // 2, (head % 2) * dim : (head % 2 + 1) * dim]
            rows = mixed[:, cols] + jnp.dot(q_feat[:, cols], state, preferred_element_type=F32)
            scale = lax.rsqrt(jnp.mean(rows * rows, axis=-1, keepdims=True) + 1e-06)
            out_buf[:, cols] = (rows * scale * gain[:, cols]).astype(BF16)

    z_lag = X_LAG + Y_LAG + Z_LAG * z
    res_lag = z_lag + R_LAG
    last_lag = jnp.maximum(res_lag + P_LAG, MIX_LAG)

    def at(step, lag, work):
        c = step - lag

        @pl.when((c >= 0) & (c < chunks))
        def _():
            work(c)

    @pl.loop(0, chunks + last_lag)
    def _(step):
        at(step, 0, states)
        at(step, X_LAG, relay_raw)
        at(step, z_lag, relay_z)
        at(step, res_lag, relay_res)
        at(step, MIX_LAG, local_mix)
        at(step, last_lag, finish)

    @pl.when(me < devices - 1)
    def _():
        remote(halo_out, halo, 0, halo_sem.at[0, 0], partner).wait_send()

    remote(x_out, x_in, 1, x_sem.at[0], partner).wait_send()
    remote(raw_out, raw_in, 2, raw_sem.at[0], across).wait_send()

    @pl.when(z < planes - 1)
    def _():
        remote(z_out, z_in, 3, z_sem.at[0], partner).wait_send()

    remote(res_out, res_in, 4, res_sem.at[0], across).wait_send()
    remote(p_out, p_out, 5, p_sem.at[0, 0], partner).wait_send()


def on_device(query_seq, key_seq, value_seq, conv_kernel, feature_map, norm_gain):
    tokens, width = query_seq.shape
    dim = feature_map.shape[0]
    devices = lax.axis_size("seq")
    chunks = width // (4 * dim)
    pieces = chunks // 3 if chunks % 3 == 0 else chunks
    rows = pltpu.VMEM((tokens, width), BF16)
    duo = pltpu.VMEM((chunks, 2 * dim, dim), BF16)
    solo = pltpu.VMEM((chunks, dim, dim), BF16)
    dma = pltpu.SemaphoreType.DMA
    hbm = pl.BlockSpec(memory_space=pl.ANY)
    vmem = pl.BlockSpec(memory_space=pltpu.VMEM)
    return pl.pallas_call(
        functools.partial(kernel, devices),
        out_shape=pltpu.MemorySpace.VMEM((tokens, width), BF16),
        in_specs=[hbm, hbm, hbm, vmem, vmem, vmem],
        out_specs=vmem,
        scratch_shapes=[
            rows,
            rows,
            rows,
            pltpu.VMEM((3, RIM, width), BF16),
            pltpu.VMEM((3, HALO, width), BF16),
            pltpu.VMEM((3, HALO, width), BF16),
            pltpu.VMEM((4, 2, RIM + tokens, LANES), F32),
            pltpu.VMEM((2 * dim, 2 * dim), BF16),
            rows,
            rows,
            rows,
            pltpu.VMEM((tokens, width), F32),
            pltpu.VMEM((chunks, 2 * dim, dim), F32),
            duo,
            duo,
            solo,
            solo,
            solo,
            solo,
            solo,
            solo,
            duo,
            pltpu.VMEM((chunks, 2, 2 * dim, dim), BF16),
            dma((3, chunks)),
            dma((3,)),
            dma((6,)),
            dma((3, pieces)),
            dma((chunks,)),
            dma((chunks,)),
            dma((chunks,)),
            dma((chunks,)),
            dma((chunks, 2)),
        ],
        compiler_params=pltpu.CompilerParams(
            collective_id=0, has_side_effects=True, vmem_limit_bytes=60 * 1024 * 1024
        ),
        name="layer",
    )(query_seq, key_seq, value_seq, conv_kernel, feature_map, norm_gain.reshape(1, width))


def solution(mesh):
    split = P(("groups", "seq"), None)
    return jax.shard_map(
        on_device,
        mesh=mesh,
        in_specs=(split, split, split, P(), P(), P()),
        out_specs=split,
        check_vma=False,
    )
```

time: 42.9 us -> 40.9 us (0.953)
  Pallas kernels: 40.8 us -> 39 us
    pallas_call x1, Pallas kernels: 40.8 us -> 39 us  [on_device(): pl.pallas_call(functools.partial(kernel, devices), out_shape=pltpu.Memory...]
where the time goes in v1:
time: 40.9 us; the launch traced here: 40.7 us
  Pallas kernels  39 us (95%)
  local copies, waits for them, and re-layouts  1.67 us (4%)
    pallas_call x1, Pallas kernels, on_device(): pl.pallas_call(functools.partial(kernel, devices), out_shape=pltpu.Memory...  39 us
    unnamed x1, local copies, waits for them, and re-layouts  1.67 us

profile of v1, /device:TPU:25, one launch (start us, length us, event | category | flops | bytes accessed | tf_op | source)
XLA Modules:
  0.0 40.7 jit_solution(6514486243384955441)
XLA Ops:
  0.0 39.0 %layer.1 = bf16[256,6144]{1,0:T(8,128)(2,1)S(1)} custom-call(bf16[256,6144]{1,0:T(8,128)(2,1)} %q_hbm.1, bf16[256,6144]{1,0:T(8,128)(2,1)} %k_hbm.1, bf16[256,6144]{1,0:T(8,128)(2,1)} %v_hbm.1, bf16[3,4,6144]{2,1,0:T(4,128)(2,1)} %taps.1, bf16[128,128]{1,0:T(8,128)(2,1)} %feature_map.1, f32[1,6144]{1,0:T(1,128)} %bitcast.1), custom_call_target="tpu_custom_call" | custom-call | tf_op jit(solution)/shard_map/layer/pallas_call | solution.py:368
  39.1 1.7 %copy.8 = bf16[256,6144]{1,0:T(8,128)(2,1)} copy(bf16[256,6144]{1,0:T(8,128)(2,1)S(1)} %layer.1) | data formatting | bytes 6291456

commit v2 on v1

--- a/solution.py
+++ b/solution.py
@@ -49,13 +49,16 @@
     q_hbm,
     k_hbm,
     v_hbm,
-    taps,
-    feature_map,
-    gain,
+    taps_hbm,
+    map_hbm,
+    gain_hbm,
     out_buf,
     q_buf,
     k_buf,
     v_buf,
+    taps,
+    feature_map,
+    gain,
     tail,
     halo_out,
     halo,
@@ -65,6 +68,7 @@
     k_feat,
     v_conv,
     mixed,
+    weights,
     own_state,
     x_out,
     x_in,
@@ -77,6 +81,7 @@
     p_out,
     prefix,
     load_sem,
+    aux_sem,
     tail_sem,
     send_sem,
     halo_sem,
@@ -111,45 +116,52 @@
         cols = pl.ds(pl.multiple_of(c * chunk, chunk), chunk)
         return pltpu.make_async_copy(sources[which].at[:, cols], buf.at[:, cols], load_sem.at[which, c])
 
-    for which in (1, 2, 0):
-        load_tail(which).start()
+    small = [
+        pltpu.make_async_copy(src, dst, aux_sem.at[n])
+        for n, (src, dst) in enumerate(((taps_hbm, taps), (map_hbm, feature_map), (gain_hbm, gain)))
+    ]
+    barrier = pltpu.get_barrier_semaphore()
+
+    def greet(target):
+        pl.semaphore_signal(barrier, inc=1, device_id={"seq": target}, device_id_type=MESH)
+
+    greet(partner)
+    greet(across)
+
+    @pl.when(me > 0)
+    def _():
+        greet(me - 1)
+
+    @pl.when(me < devices - 1)
+    def _():
+        greet(me + 1)
+
+    @pl.when(z > 0)
+    def _():
+        greet(me - 4)
+
+    @pl.when(z < planes - 1)
+    def _():
+        greet(me + 4)
+
+    load_tail(1).start()
+    load_tail(2).start()
+    small[0].start()
+    small[1].start()
 
     @pl.loop(0, chunks)
     def _(c):
         load(k_buf, 1, c).start()
         load(v_buf, 2, c).start()
 
-    barrier = pltpu.get_barrier_semaphore()
-
-    def greet(target):
-        pl.semaphore_signal(barrier, inc=1, device_id={"seq": target}, device_id_type=MESH)
-
-    greet(partner)
-    greet(across)
-
-    @pl.when(me > 0)
-    def _():
-        greet(me - 1)
-
-    @pl.when(me < devices - 1)
-    def _():
-        greet(me + 1)
-
-    @pl.when(z > 0)
-    def _():
-        greet(me - 4)
-
-    @pl.when(z < planes - 1)
-    def _():
-        greet(me + 4)
+    load_tail(0).start()
+    small[2].start()
 
     @pl.loop(0, chunks)
     def _(c):
         load(q_buf, 0, c).start()
 
     wide_map[...] = jnp.zeros_like(wide_map)
-    wide_map[:dim, :dim] = feature_map[...]
-    wide_map[dim:, dim:] = feature_map[...]
 
     @pl.when(me == 0)
     def _():
@@ -164,6 +176,11 @@
     for which in (1, 2, 0):
         load_tail(which).wait()
         halo_out[which] = tail[which].astype(F32)[RIM - HALO :].astype(BF16)
+
+    small[0].wait()
+    small[1].wait()
+    wide_map[:dim, :dim] = feature_map[...]
+    wide_map[dim:, dim:] = feature_map[...]
 
     edges = [(me > 0), (me < devices - 1), (z > 0), (z < planes - 1)]
     pl.semaphore_wait(barrier, 2 + sum(e.astype(jnp.int32) for e in edges))
@@ -225,25 +242,33 @@
         rows = pl.ds(pl.multiple_of(h * dim, dim), dim)
         return remote(p_out.at[c, rows], prefix.at[c, core, rows], 5, p_sem.at[c, h], partner)
 
+    def pair_state(feat, v_rows):
+        both = lax.dot_general(feat, v_rows, (((0,), (0,)), ((), ())), preferred_element_type=F32)
+        return both[:dim, :dim], both[dim:, dim:]
+
+    def keep_own(c):
+        cols = pl.ds(pl.multiple_of(c * chunk + core * pair, pair), pair)
+        first, second = pair_state(k_feat[:, cols], v_conv[:, cols])
+        own_state[c, :dim] = first
+        own_state[c, dim:] = second
+
     def states(c):
         load(k_buf, 1, c).wait()
         load(v_buf, 2, c).wait()
         wait_halo(c, (1, 2))
-        found = []
+        keep_own(jnp.maximum(c - 1, 0))
         for side in range(2):
             turn = 1 - core if side == 0 else core
             col = pl.multiple_of(c * chunk + turn * pair, pair)
             k_rows = short_conv(k_buf, halo, taps, 1, col, pair, wide.at[2 * side])
+            feat = features(k_rows, wide_map)
             v_rows = short_conv(v_buf, halo, taps, 2, col, pair, wide.at[2 * side + 1])
-            feat = features(k_rows, wide_map)
             k_feat[:, pl.ds(col, pair)] = feat
             v_conv[:, pl.ds(col, pair)] = v_rows
-            both = lax.dot_general(feat, v_rows, (((0,), (0,)), ((), ())), preferred_element_type=F32)
-            found.append((both[:dim, :dim], both[dim:, dim:]))
-        x_out[c, :dim] = found[0][0].astype(BF16)
-        x_out[c, dim:] = found[0][1].astype(BF16)
-        own_state[c, :dim] = found[1][0]
-        own_state[c, dim:] = found[1][1]
+            if side == 0:
+                first, second = pair_state(feat, v_rows)
+                x_out[c, :dim] = first.astype(BF16)
+                x_out[c, dim:] = second.astype(BF16)
         x_copy(c).start()
 
     def relay_raw(c):
@@ -274,39 +299,52 @@
             z_copy(c).start()
 
         res_out[c] = (before + jnp.where(y == 0, chip, 0.0)).astype(BF16)
+        hand_on(c, y, lead, before + jnp.where(y == 1, far, 0.0))
+
+    def send_res(c):
         res_copy(c).start()
-        hand_on(c, y, lead, before + jnp.where(y == 1, far, 0.0))
 
     def relay_res(c):
         res_copy(c).wait_recv()
         hand_on(c, 1 - y, other, res_in[c].astype(F32))
 
-    def local_mix(c):
-        load(q_buf, 0, c).wait()
-        wait_halo(c, (0,))
-        row = lax.broadcasted_iota(jnp.int32, (half, half), 0)
-        causal = row >= lax.broadcasted_iota(jnp.int32, (half, half), 1)
+    def mix_values(c):
+        for head in range(4):
+            cols = pl.ds(pl.multiple_of(c * chunk + head * dim, dim), dim)
+            values = v_conv[:, cols]
+            mixed[:half, cols] = jnp.dot(weights[head, :half, :half], values[:half], preferred_element_type=F32)
+            mixed[half:, cols] = jnp.dot(weights[head, half:], values, preferred_element_type=F32)
+
+    def query(c):
         for side in range(2):
             col = pl.multiple_of(c * chunk + side * pair, pair)
             q_rows = short_conv(q_buf, halo, taps, 0, col, pair, wide.at[side])
-            feat = features(q_rows, wide_map)
-            q_feat[:, pl.ds(col, pair)] = feat
-            for head in range(2):
-                cols = pl.ds(pl.multiple_of(col + head * dim, dim), dim)
-                scores = lax.dot_general(
-                    feat[:, head * dim : (head + 1) * dim],
-                    k_feat[:, cols],
-                    (((1,), (1,)), ((), ())),
-                    preferred_element_type=F32,
-                )
-                upper = jnp.where(causal, scores[:half, :half], 0.0).astype(BF16)
-                left = scores[half:, :half].astype(BF16)
-                lower = jnp.where(causal, scores[half:, half:], 0.0).astype(BF16)
-                values = v_conv[:, cols]
-                mixed[:half, cols] = jnp.dot(upper, values[:half], preferred_element_type=F32)
-                mixed[half:, cols] = jnp.dot(
-                    jnp.concatenate([left, lower], axis=1), values, preferred_element_type=F32
-                )
+            q_feat[:, pl.ds(col, pair)] = features(q_rows, wide_map)
+
+    def mix_scores(c):
+        row = lax.broadcasted_iota(jnp.int32, (half, half), 0)
+        causal = row >= lax.broadcasted_iota(jnp.int32, (half, half), 1)
+        for head in range(4):
+            cols = pl.ds(pl.multiple_of(c * chunk + head * dim, dim), dim)
+            scores = lax.dot_general(
+                q_feat[:, cols], k_feat[:, cols], (((1,), (1,)), ((), ())), preferred_element_type=F32
+            )
+            place = weights.at[head]
+            place[:half, :half] = jnp.where(causal, scores[:half, :half], 0.0).astype(BF16)
+            place[half:, :half] = scores[half:, :half].astype(BF16)
+            place[half:, half:] = jnp.where(causal, scores[half:, half:], 0.0).astype(BF16)
+
+    def await_query(c):
+        @pl.when(c < chunks)
+        def _():
+            load(q_buf, 0, c).wait()
+            wait_halo(c, (0,))
+
+    def local_mix(c):
+        await_query(c + 1)
+        mix_values(jnp.maximum(c - 1, 0))
+        mix_scores(c)
+        query(jnp.minimum(c + 1, chunks - 1))
 
     def finish(c):
         p_copy(c, 0).wait_recv()
@@ -319,8 +357,9 @@
             out_buf[:, cols] = (rows * scale * gain[:, cols]).astype(BF16)
 
     z_lag = X_LAG + Y_LAG + Z_LAG * z
-    res_lag = z_lag + R_LAG
-    last_lag = jnp.maximum(res_lag + P_LAG, MIX_LAG)
+    send_lag = jnp.maximum(z_lag, chunks + X_LAG)
+    res_lag = send_lag + R_LAG
+    last_lag = jnp.maximum(res_lag + P_LAG, MIX_LAG + 1)
 
     def at(step, lag, work):
         c = step - lag
@@ -332,10 +371,26 @@
     @pl.loop(0, chunks + last_lag)
     def _(step):
         at(step, 0, states)
+        @pl.when(step == chunks)
+        def _():
+            keep_own(chunks - 1)
+
         at(step, X_LAG, relay_raw)
         at(step, z_lag, relay_z)
+        at(step, send_lag, send_res)
         at(step, res_lag, relay_res)
+        @pl.when(step == MIX_LAG - 1)
+        def _():
+            small[2].wait()
+            await_query(0)
+            query(0)
+
         at(step, MIX_LAG, local_mix)
+
+        @pl.when(step == MIX_LAG + chunks)
+        def _():
+            mix_values(chunks - 1)
+
         at(step, last_lag, finish)
 
     @pl.when(me < devices - 1)
@@ -368,12 +423,15 @@
     return pl.pallas_call(
         functools.partial(kernel, devices),
         out_shape=pltpu.MemorySpace.VMEM((tokens, width), BF16),
-        in_specs=[hbm, hbm, hbm, vmem, vmem, vmem],
+        in_specs=[hbm] * 6,
         out_specs=vmem,
         scratch_shapes=[
             rows,
             rows,
             rows,
+            pltpu.VMEM(conv_kernel.shape, BF16),
+            pltpu.VMEM(feature_map.shape, BF16),
+            pltpu.VMEM((1, width), F32),
             pltpu.VMEM((3, RIM, width), BF16),
             pltpu.VMEM((3, HALO, width), BF16),
             pltpu.VMEM((3, HALO, width), BF16),
@@ -383,6 +441,7 @@
             rows,
             rows,
             pltpu.VMEM((tokens, width), F32),
+            pltpu.VMEM((4, tokens, tokens), BF16),
             pltpu.VMEM((chunks, 2 * dim, dim), F32),
             duo,
             duo,
@@ -395,6 +454,7 @@
             duo,
             pltpu.VMEM((chunks, 2, 2 * dim, dim), BF16),
             dma((3, chunks)),
+            dma((3,)),
             dma((3,)),
             dma((6,)),
             dma((3, pieces)),

time: 40.9 us -> 36.9 us (0.902)
  Pallas kernels: 39 us -> 35.1 us
    pallas_call x1, Pallas kernels: 39 us -> 35.1 us  [on_device(): pl.pallas_call(functools.partial(kernel, devices), out_shape=pltpu.Memory...]
where the time goes in v2:
time: 36.9 us; the launch traced here: 36.7 us
  Pallas kernels  35.1 us (95%)
  local copies, waits for them, and re-layouts  1.67 us (5%)
    pallas_call x1, Pallas kernels, on_device(): pl.pallas_call(functools.partial(kernel, devices), out_shape=pltpu.Memory...  35.1 us
    unnamed x1, local copies, waits for them, and re-layouts  1.67 us

profile of v2, /device:TPU:25, one launch (start us, length us, event | category | flops | bytes accessed | tf_op | source)
XLA Modules:
  0.0 36.7 jit_solution(5863272141441088800)
XLA Ops:
  0.0 35.1 %layer.1 = bf16[256,6144]{1,0:T(8,128)(2,1)S(1)} custom-call(bf16[256,6144]{1,0:T(8,128)(2,1)} %q_hbm.1, bf16[256,6144]{1,0:T(8,128)(2,1)} %k_hbm.1, bf16[256,6144]{1,0:T(8,128)(2,1)} %v_hbm.1, bf16[3,4,6144]{2,1,0:T(4,128)(2,1)} %taps_hbm.1, bf16[128,128]{1,0:T(8,128)(2,1)} %map_hbm.1, f32[1,6144]{1,0:T(1,128)} %bitcast.1), custom_call_target="tpu_custom_call" | custom-call | tf_op jit(solution)/shard_map/layer/pallas_call | solution.py:423
  35.1 1.7 %copy.8 = bf16[256,6144]{1,0:T(8,128)(2,1)} copy(bf16[256,6144]{1,0:T(8,128)(2,1)S(1)} %layer.1) | data formatting | bytes 6291456

commit v3 on v2

v3 whole, which is shorter than its diff:
```python
import functools

import jax
import jax.numpy as jnp
from jax import lax
from jax.experimental import pallas as pl
from jax.experimental.pallas import tpu as pltpu
from jax.sharding import PartitionSpec as P

MESH = pl.DeviceIdType.MESH
F32 = jnp.float32
BF16 = jnp.bfloat16
RIM = 8
HALO = 4
LANES = 128
X_LAG = 2
Y_LAG = 4
Z_LAG = 3
R_LAG = 3
P_LAG = 2
MIX_LAG = 11
LAST_MIX_LAG = 9
TAIL = 2


def short_conv(buf, halo, taps, which, col, width, wide):
    tap_count = taps.shape[1]
    length = buf.shape[0]
    out = []
    for j in range(width // LANES):
        lanes = pl.ds(pl.multiple_of(col + j * LANES, LANES), LANES)
        tall = wide.at[j]
        tap_rows = taps[which, :, lanes].astype(F32)
        tall[RIM - HALO : RIM] = halo[which, :, lanes].astype(F32)
        rows = buf[:, lanes].astype(F32)
        tall[RIM:] = rows
        total = tap_rows[0:1] * rows
        for offset in range(1, tap_count):
            total = total + tap_rows[offset : offset + 1] * tall[RIM - offset : RIM - offset + length]
        out.append(total.astype(BF16))
    return jnp.concatenate(out, axis=1)


def features(conv_rows, wide_map):
    projected = jnp.dot(conv_rows, wide_map[...], preferred_element_type=F32)
    return jnp.where(projected > 0, projected + 1.0, jnp.exp(projected)).astype(BF16)


def put_pair(buf, first, rows):
    dim = buf.shape[2]
    buf[first] = rows[:, :dim]
    buf[first + 1] = rows[:, dim:]


def get_pair(buf, first):
    return jnp.concatenate([buf[first], buf[first + 1]], axis=1)


def fill_average(average):
    dim = average.shape[0] // 2
    average[...] = jnp.zeros_like(average)
    average[:dim, :dim] = jnp.full((dim, dim), 1.0 / dim, BF16)
    average[dim:, dim:] = jnp.full((dim, dim), 1.0 / dim, BF16)


def normalize(c, out, first, mixed, q_feat, prefix, gain, total, squares, average):
    pair = average.shape[0]
    spans = [pl.ds(pl.multiple_of((2 * c + side) * pair, pair), pair) for side in range(2)]
    for side in range(2):
        query = get_pair(q_feat, 4 * c + 2 * side)
        rows = mixed[:, spans[side]] + jnp.dot(query, prefix[c, side], preferred_element_type=F32)
        total[side] = rows
        squares[side] = (rows * rows).astype(BF16)
    for side in range(2):
        mean = jnp.dot(squares[side], average[...], preferred_element_type=F32)
        done = (total[side] * lax.rsqrt(mean + 1e-06) * gain[:, spans[side]]).astype(BF16)
        put_pair(out, first + 2 * side, done)


def kernel(
    devices,
    q_hbm,
    k_hbm,
    v_hbm,
    taps_hbm,
    map_hbm,
    gain_hbm,
    out_buf,
    mixed,
    q_feat,
    prefix,
    gain,
    q_buf,
    k_buf,
    v_buf,
    taps,
    feature_map,
    tail,
    halo_out,
    halo,
    wide,
    wide_map,
    q_stage,
    k_feat,
    v_conv,
    weights,
    total,
    squares,
    average,
    own_state,
    x_out,
    x_in,
    raw_out,
    raw_in,
    z_out,
    z_in,
    res_out,
    res_in,
    p_out,
    load_sem,
    aux_sem,
    tail_sem,
    send_sem,
    halo_sem,
    x_sem,
    raw_sem,
    z_sem,
    res_sem,
    p_sem,
):
    tokens, width = q_buf.shape
    half = tokens // 2
    dim = feature_map.shape[0]
    pair = 2 * dim
    chunk = 2 * pair
    chunks = width // chunk
    me = lax.axis_index("seq")
    core = lax.rem(me, 2)
    y = lax.rem(me // 2, 2)
    z = me // 4
    planes = devices // 4
    partner = me + 1 - 2 * core
    across = me + 2 - 4 * y
    sources = (q_hbm, k_hbm, v_hbm)

    def load_tail(which):
        rows = pl.ds(tokens - RIM, RIM)
        return pltpu.make_async_copy(sources[which].at[rows], tail.at[which], tail_sem.at[which])

    def load(buf, which, c):
        cols = pl.ds(pl.multiple_of(c * chunk, chunk), chunk)
        return pltpu.make_async_copy(sources[which].at[:, cols], buf.at[:, cols], load_sem.at[which, c])

    small = [
        pltpu.make_async_copy(src, dst, aux_sem.at[n])
        for n, (src, dst) in enumerate(((taps_hbm, taps), (map_hbm, feature_map), (gain_hbm, gain)))
    ]
    barrier = pltpu.get_barrier_semaphore()

    def greet(target):
        pl.semaphore_signal(barrier, inc=1, device_id={"seq": target}, device_id_type=MESH)

    greet(partner)
    greet(across)

    @pl.when(me > 0)
    def _():
        greet(me - 1)

    @pl.when(me < devices - 1)
    def _():
        greet(me + 1)

    @pl.when(z > 0)
    def _():
        greet(me - 4)

    @pl.when(z < planes - 1)
    def _():
        greet(me + 4)

    load_tail(1).start()
    load_tail(2).start()
    small[0].start()
    small[1].start()

    def load_pair(c):
        load(k_buf, 1, c).start()
        load(v_buf, 2, c).start()

    load_pair(0)
    load_pair(1)

    wide_map[...] = jnp.zeros_like(wide_map)
    fill_average(average)

    @pl.when(me == 0)
    def _():
        halo[...] = jnp.zeros_like(halo)

    @pl.when(z == 0)
    def _():
        @pl.loop(0, chunks)
        def _(c):
            z_in[c] = jnp.zeros(z_in.shape[1:], BF16)

    def ready_tail(which):
        load_tail(which).wait()
        halo_out[which] = tail[which].astype(F32)[RIM - HALO :].astype(BF16)

    ready_tail(1)
    ready_tail(2)
    small[0].wait()
    small[1].wait()
    wide_map[:dim, :dim] = feature_map[...]
    wide_map[dim:, dim:] = feature_map[...]

    edges = [(me > 0), (me < devices - 1), (z > 0), (z < planes - 1)]
    pl.semaphore_wait(barrier, 2 + sum(e.astype(jnp.int32) for e in edges))

    def remote(src, dst, kind, recv_sem, target):
        return pltpu.make_async_remote_copy(
            src_ref=src,
            dst_ref=dst,
            send_sem=send_sem.at[kind],
            recv_sem=recv_sem,
            device_id={"seq": target},
            device_id_type=MESH,
        )

    def halo_copy(which, piece):
        cols = pl.ds(0, chunk) if piece == 0 else pl.ds(chunk, width - chunk)
        return remote(
            halo_out.at[which, :, cols],
            halo.at[which, :, cols],
            0,
            halo_sem.at[which, piece],
            lax.rem(me + 1, devices),
        )

    @pl.when(me < devices - 1)
    def _():
        for piece in range(2):
            for which in (1, 2):
                halo_copy(which, piece).start()

    load_tail(0).start()
    small[2].start()

    @pl.loop(2, chunks)
    def _(c):
        load_pair(c)

    @pl.loop(0, chunks)
    def _(c):
        load(q_buf, 0, c).start()

    @pl.loop(0, chunks)
    def _(c):
        blank = jnp.zeros((dim, dim), BF16)
        for side in range(2):
            prefix[c, side, :dim, dim:] = blank
            prefix[c, side, dim:, :dim] = blank

    ready_tail(0)

    @pl.when(me < devices - 1)
    def _():
        for piece in range(2):
            halo_copy(0, piece).start()

    def wait_halo(c, which):
        for piece in range(2):

            @pl.when((me > 0) & (c == piece))
            def _():
                for w in which:
                    halo_copy(w, piece).wait_recv()

    lead = pl.ds(pl.multiple_of(y * dim, dim), dim)
    other = pl.ds(pl.multiple_of((1 - y) * dim, dim), dim)

    def x_copy(c):
        return remote(x_out.at[c], x_in.at[c], 1, x_sem.at[c], partner)

    def raw_copy(c):
        return remote(raw_out.at[c], raw_in.at[c], 2, raw_sem.at[c], across)

    def z_copy(c):
        return remote(z_out.at[c], z_in.at[c], 3, z_sem.at[c], lax.rem(me + 4, devices))

    def res_copy(c):
        return remote(res_out.at[c], res_in.at[c], 4, res_sem.at[c], across)

    def p_copy(c, h):
        rows = pl.ds(pl.multiple_of(h * dim, dim), dim)
        return remote(p_out.at[c, rows], prefix.at[c, core, rows, rows], 5, p_sem.at[c, h], partner)

    def pair_state(feat, v_rows):
        both = lax.dot_general(feat, v_rows, (((0,), (0,)), ((), ())), preferred_element_type=F32)
        return both[:dim, :dim], both[dim:, dim:]

    def keep_own(c):
        first_head = 4 * c + 2 * core
        first, second = pair_state(get_pair(k_feat, first_head), get_pair(v_conv, first_head))
        own_state[c, :dim] = first
        own_state[c, dim:] = second

    def states(c):
        load(k_buf, 1, c).wait()
        load(v_buf, 2, c).wait()
        wait_halo(c, (1, 2))
        keep_own(jnp.maximum(c - 1, 0))
        turns = (1 - core, core)
        heads = [4 * c + 2 * turn for turn in turns]
        cols = [pl.multiple_of(c * chunk + turn * pair, pair) for turn in turns]

        def key_rows(side):
            return short_conv(k_buf, halo, taps, 1, cols[side], pair, wide.at[2 * side])

        def value_rows(side):
            return short_conv(v_buf, halo, taps, 2, cols[side], pair, wide.at[2 * side + 1])

        key_0 = key_rows(0)
        feat_0 = features(key_0, wide_map)
        key_1 = key_rows(1)
        put_pair(k_feat, heads[0], feat_0)
        values_0 = value_rows(0)
        put_pair(v_conv, heads[0], values_0)
        put_pair(k_feat, heads[1], features(key_1, wide_map))
        first, second = pair_state(feat_0, values_0)
        put_pair(v_conv, heads[1], value_rows(1))
        x_out[c, :dim] = first.astype(BF16)
        x_out[c, dim:] = second.astype(BF16)
        x_copy(c).start()

    def relay_raw(c):
        x_copy(c).wait_recv()
        raw_out[c] = (own_state[c, other] + x_in[c, other].astype(F32)).astype(BF16)
        raw_copy(c).start()

    def hand_on(c, h, rows, earlier):
        p_out[c, rows] = (earlier + jnp.where(core == 0, own_state[c, rows], 0.0)).astype(BF16)
        p_copy(c, h).start()
        own = earlier + jnp.where(core == 1, x_in[c, rows].astype(F32), 0.0)
        prefix[c, core, rows, rows] = own.astype(BF16)

    z_lag = X_LAG + Y_LAG + Z_LAG * z
    raw_end = chunks + X_LAG

    def relay_z(c):
        raw_copy(c).wait_recv()

        @pl.when(z > 0)
        def _():
            z_copy(c).wait_recv()

        before = z_in[c].astype(F32)
        chip = own_state[c, lead] + x_in[c, lead].astype(F32)
        far = raw_in[c].astype(F32)
        z_out[c] = (before + chip + far).astype(BF16)

        @pl.when(z < planes - 1)
        def _():
            z_copy(c).start()

        res_out[c] = (before + jnp.where(y == 0, chip, 0.0)).astype(BF16)

        @pl.when(c + z_lag >= raw_end)
        def _():
            res_copy(c).start()

        hand_on(c, y, lead, before + jnp.where(y == 1, far, 0.0))

    def relay_res(c):
        res_copy(c).wait_recv()
        hand_on(c, 1 - y, other, res_in[c].astype(F32))

    def mix_values(c, head):
        cols = pl.ds(pl.multiple_of(c * chunk + head * dim, dim), dim)
        values = v_conv[4 * c + head]
        mixed[:half, cols] = jnp.dot(weights[head, :half, :half], values[:half], preferred_element_type=F32)
        mixed[half:, cols] = jnp.dot(weights[head, half:], values, preferred_element_type=F32)

    def query_rows(c, side):
        return short_conv(q_buf, halo, taps, 0, c * chunk + side * pair, pair, wide.at[side])

    def query_feat(c, side, rows):
        feat = features(rows, wide_map)
        put_pair(q_stage, 2 * side, feat)
        put_pair(q_feat, 4 * c + 2 * side, feat)

    def mix_scores(c, head):
        row = lax.broadcasted_iota(jnp.int32, (half, half), 0)
        causal = row >= lax.broadcasted_iota(jnp.int32, (half, half), 1)
        scores = lax.dot_general(
            q_stage[head],
            k_feat[4 * c + head],
            (((1,), (1,)), ((), ())),
            preferred_element_type=F32,
        )
        place = weights.at[head]
        place[:half, :half] = jnp.where(causal, scores[:half, :half], 0.0).astype(BF16)
        place[half:, :half] = scores[half:, :half].astype(BF16)
        place[half:, half:] = jnp.where(causal, scores[half:, half:], 0.0).astype(BF16)

    def await_query(c):
        @pl.when(c < chunks)
        def _():
            load(q_buf, 0, c).wait()
            wait_halo(c, (0,))

    def local_mix(c):
        await_query(c + 1)
        last = jnp.maximum(c - 1, 0)
        after = jnp.minimum(c + 1, chunks - 1)
        for side in range(2):
            rows = query_rows(after, side)
            mix_values(last, 2 * side)
            mix_values(last, 2 * side + 1)
            mix_scores(c, 2 * side)
            mix_scores(c, 2 * side + 1)
            query_feat(after, side, rows)

    def finish(c):
        p_copy(c, 0).wait_recv()
        p_copy(c, 1).wait_recv()

        @pl.when(c < chunks - TAIL)
        def _():
            normalize(c, out_buf, 4 * c, mixed, q_feat, prefix, gain, total, squares, average)

    res_lag = jnp.maximum(z_lag, raw_end) + R_LAG
    mix_lag = jnp.where(z == planes - 1, LAST_MIX_LAG, MIX_LAG)
    last_lag = jnp.maximum(res_lag + P_LAG, mix_lag + 1)

    def at(step, lag, work):
        c = step - lag

        @pl.when((c >= 0) & (c < chunks))
        def _():
            work(c)

    @pl.loop(0, chunks + last_lag)
    def _(step):
        at(step, 0, states)
        @pl.when(step == chunks)
        def _():
            keep_own(chunks - 1)

        at(step, X_LAG, relay_raw)

        @pl.when(step == raw_end)
        def _():
            @pl.loop(0, jnp.maximum(raw_end - z_lag, 0))
            def _(c):
                res_copy(c).start()

        at(step, z_lag, relay_z)
        at(step, res_lag, relay_res)
        @pl.when(step == mix_lag - 1)
        def _():
            small[2].wait()
            await_query(0)
            for side in range(2):
                query_feat(0, side, query_rows(0, side))

        at(step, mix_lag, local_mix)

        @pl.when(step == mix_lag + chunks)
        def _():
            for head in range(4):
                mix_values(chunks - 1, head)

        at(step, last_lag, finish)

    @pl.when(me < devices - 1)
    def _():
        remote(halo_out, halo, 0, halo_sem.at[0, 0], partner).wait_send()

    remote(x_out, x_in, 1, x_sem.at[0], partner).wait_send()
    remote(raw_out, raw_in, 2, raw_sem.at[0], across).wait_send()

    @pl.when(z < planes - 1)
    def _():
        remote(z_out, z_in, 3, z_sem.at[0], partner).wait_send()

    remote(res_out, res_in, 4, res_sem.at[0], across).wait_send()
    remote(p_out, p_out, 5, p_sem.at[0, 0], partner).wait_send()


def store(done, mixed, q_feat, prefix, gain, out, late, total, squares, average, sem):
    heads, _, dim = done.shape
    chunks = heads // 4
    ready = chunks - TAIL

    def copy(src, h):
        cols = pl.ds(pl.multiple_of(h * dim, dim), dim)
        return pltpu.make_async_copy(src, out.at[:, cols], sem.at[0])

    @pl.loop(0, 4 * ready)
    def _(h):
        copy(done.at[h], h).start()

    fill_average(average)

    @pl.loop(0, TAIL)
    def _(n):
        normalize(ready + n, late, 4 * n, mixed, q_feat, prefix, gain, total, squares, average)
        for h in range(4):
            copy(late.at[4 * n + h], 4 * (ready + n) + h).start()

    pltpu.make_async_copy(out, out, sem.at[0]).wait()


def on_device(query_seq, key_seq, value_seq, conv_kernel, feature_map, norm_gain):
    tokens, width = query_seq.shape
    dim = feature_map.shape[0]
    devices = lax.axis_size("seq")
    chunks = width // (4 * dim)
    rows = pltpu.VMEM((tokens, width), BF16)
    heads = pltpu.VMEM((width // dim, tokens, dim), BF16)
    duo = pltpu.VMEM((chunks, 2 * dim, dim), BF16)
    solo = pltpu.VMEM((chunks, dim, dim), BF16)
    dma = pltpu.SemaphoreType.DMA
    keep = pltpu.MemorySpace.VMEM
    hbm = pl.BlockSpec(memory_space=pl.ANY)
    vmem = pl.BlockSpec(memory_space=pltpu.VMEM)
    parts = pl.pallas_call(
        functools.partial(kernel, devices),
        out_shape=[
            keep((width // dim, tokens, dim), BF16),
            keep((tokens, width), F32),
            keep((width // dim, tokens, dim), BF16),
            keep((chunks, 2, 2 * dim, 2 * dim), BF16),
            keep((1, width), F32),
        ],
        in_specs=[hbm] * 6,
        out_specs=[vmem] * 5,
        scratch_shapes=[
            rows,
            rows,
            rows,
            pltpu.VMEM(conv_kernel.shape, BF16),
            pltpu.VMEM(feature_map.shape, BF16),
            pltpu.VMEM((3, RIM, width), BF16),
            pltpu.VMEM((3, HALO, width), BF16),
            pltpu.VMEM((3, HALO, width), BF16),
            pltpu.VMEM((4, 2, RIM + tokens, LANES), F32),
            pltpu.VMEM((2 * dim, 2 * dim), BF16),
            pltpu.VMEM((4, tokens, dim), BF16),
            heads,
            heads,
            pltpu.VMEM((4, tokens, tokens), BF16),
            pltpu.VMEM((2, tokens, 2 * dim), F32),
            pltpu.VMEM((2, tokens, 2 * dim), BF16),
            pltpu.VMEM((2 * dim, 2 * dim), BF16),
            pltpu.VMEM((chunks, 2 * dim, dim), F32),
            duo,
            duo,
            solo,
            solo,
            solo,
            solo,
            solo,
            solo,
            duo,
            dma((3, chunks)),
            dma((3,)),
            dma((3,)),
            dma((6,)),
            dma((3, 2)),
            dma((chunks,)),
            dma((chunks,)),
            dma((chunks,)),
            dma((chunks,)),
            dma((chunks, 2)),
        ],
        compiler_params=pltpu.CompilerParams(
            collective_id=0, has_side_effects=True, vmem_limit_bytes=40 * 1024 * 1024
        ),
        name="layer",
    )(query_seq, key_seq, value_seq, conv_kernel, feature_map, norm_gain.reshape(1, width))
    return pl.pallas_call(
        store,
        out_shape=jax.ShapeDtypeStruct((tokens, width), BF16),
        in_specs=[vmem] * 5,
        out_specs=hbm,
        scratch_shapes=[
            pltpu.VMEM((4 * TAIL, tokens, dim), BF16),
            pltpu.VMEM((2, tokens, 2 * dim), F32),
            pltpu.VMEM((2, tokens, 2 * dim), BF16),
            pltpu.VMEM((2 * dim, 2 * dim), BF16),
            dma((1,)),
        ],
        compiler_params=pltpu.CompilerParams(vmem_limit_bytes=8 * 1024 * 1024),
        name="store",
    )(*parts)


def solution(mesh):
    split = P(("groups", "seq"), None)
    return jax.shard_map(
        on_device,
        mesh=mesh,
        in_specs=(split, split, split, P(), P(), P()),
        out_specs=split,
        check_vma=False,
    )
```

time: 36.9 us -> 34.5 us (0.935)
  local copies, waits for them, and re-layouts: 1.67 us -> 0 us
  Pallas kernels: 35.1 us -> 34.3 us
    unnamed x1 -> x0, local copies, waits for them, and re-layouts: 1.67 us -> none
    pallas_call x1 -> x2, Pallas kernels: 35.1 us -> 34.3 us  [the longest x1 32.5 us: on_device(): pl.pallas_call(functools.partial(kernel, devices), out_shape=[keep((width...]
where the time goes in v3:
time: 34.5 us; the launch traced here: 34.3 us
  Pallas kernels  34.3 us (99%)
    pallas_call x1, Pallas kernels, on_device(): pl.pallas_call(functools.partial(kernel, devices), out_shape=[keep((width...  32.5 us
    pallas_call x1, Pallas kernels, on_device(): pl.pallas_call(store, out_shape=jax.ShapeDtypeStruct((tokens, width), BF1...  1.83 us

profile of v3, /device:TPU:25, one launch (start us, length us, event | category | flops | bytes accessed | tf_op | source)
XLA Modules:
  0.0 34.3 jit_solution(10837211733069238662)
XLA Ops:
  0.0 32.5 %layer.1 = (bf16[48,256,128]{2,1,0:T(8,128)(2,1)S(1)}, f32[256,6144]{1,0:T(8,128)S(1)}, bf16[48,256,128]{2,1,0:T(8,128)(2,1)S(1)}, bf16[12,2,256,256]{3,2,1,0:T(8,128)(2,1)S(1)}, f32[1,6144]{1,0:T(1,128)S(1)}) custom-call(bf16[256,6144]{1,0:T(8,128)(2,1)} %q_hbm.1, bf16[256,6144]{1,0:T(8,128)(2,1)} %k_hbm.1, bf16[256,6144]{1,0:T(8,128)(2,1)} %v_hbm.1, ...), custom_call_target="tpu_custom_call" | custom-call | tf_op jit(solution)/shard_map/layer/pallas_call | solution.py:529
  32.5 1.8 %store.1 = bf16[256,6144]{1,0:T(8,128)(2,1)} custom-call(bf16[48,256,128]{2,1,0:T(8,128)(2,1)S(1)} %get-tuple-element.10.done, f32[256,6144]{1,0:T(8,128)S(1)} %get-tuple-element.11.mixed, bf16[48,256,128]{2,1,0:T(8,128)(2,1)S(1)} %get-tuple-element.12.q_feat, bf16[12,2,256,256]{3,2,1,0:T(8,128)(2,1)S(1)} %get-tuple-element.13.prefix, ...), custom_call_target="tpu_custom_call" | custom-call | tf_op jit(solution)/shard_map/store/pallas_call | solution.py:584

commit v4 on v3

--- a/solution.py
+++ b/solution.py
@@ -16,8 +16,11 @@
 X_LAG = 2
 Y_LAG = 4
 Z_LAG = 3
-R_LAG = 3
-P_LAG = 2
+R_LAG = 5
+P_LAG = 3
+CATCH_ONE = 2
+CATCH_TWO = 5
+CATCH_PLANE = 3
 MIX_LAG = 11
 LAST_MIX_LAG = 9
 TAIL = 2
@@ -348,7 +351,7 @@
     z_lag = X_LAG + Y_LAG + Z_LAG * z
     raw_end = chunks + X_LAG
 
-    def relay_z(c):
+    def relay_z(c, step):
         raw_copy(c).wait_recv()
 
         @pl.when(z > 0)
@@ -366,7 +369,7 @@
 
         res_out[c] = (before + jnp.where(y == 0, chip, 0.0)).astype(BF16)
 
-        @pl.when(c + z_lag >= raw_end)
+        @pl.when(step >= raw_end)
         def _():
             res_copy(c).start()
 
@@ -430,9 +433,20 @@
         def _():
             normalize(c, out_buf, 4 * c, mixed, q_feat, prefix, gain, total, squares, average)
 
-    res_lag = jnp.maximum(z_lag, raw_end) + R_LAG
     mix_lag = jnp.where(z == planes - 1, LAST_MIX_LAG, MIX_LAG)
-    last_lag = jnp.maximum(res_lag + P_LAG, mix_lag + 1)
+    catch = 1 + (z >= CATCH_PLANE).astype(jnp.int32)
+    last_lag = jnp.maximum(jnp.maximum(raw_end, z_lag - catch) + R_LAG + P_LAG, mix_lag + 1)
+
+    def sums_by(step):
+        one = (step >= chunks + CATCH_ONE).astype(jnp.int32)
+        two = ((step >= chunks + CATCH_TWO) & (z >= CATCH_PLANE)).astype(jnp.int32)
+        return jnp.clip(step - z_lag + 1 + one + two, 0, chunks)
+
+    def results_by(step):
+        return jnp.minimum(sums_by(step - R_LAG), jnp.clip(step - raw_end - R_LAG + 1, 0, chunks))
+
+    def finished_by(step):
+        return jnp.minimum(results_by(step - P_LAG), jnp.clip(step - mix_lag, 0, chunks))
 
     def at(step, lag, work):
         c = step - lag
@@ -452,12 +466,15 @@
 
         @pl.when(step == raw_end)
         def _():
-            @pl.loop(0, jnp.maximum(raw_end - z_lag, 0))
+            @pl.loop(0, sums_by(step - 1))
             def _(c):
                 res_copy(c).start()
 
-        at(step, z_lag, relay_z)
-        at(step, res_lag, relay_res)
+        @pl.loop(sums_by(step - 1), sums_by(step))
+        def _(c):
+            relay_z(c, step)
+
+        at(step, jnp.maximum(raw_end, z_lag - catch) + R_LAG, relay_res)
         @pl.when(step == mix_lag - 1)
         def _():
             small[2].wait()

time: 34.5 us -> 32.8 us (0.951)
  Pallas kernels: 34.3 us -> 32.6 us
    pallas_call x1, Pallas kernels: 32.5 us -> 30.8 us  [on_device(): pl.pallas_call(functools.partial(kernel, devices), out_shape=[keep((width...]
where the time goes in v4:
time: 32.8 us; the launch traced here: 32.6 us
  Pallas kernels  32.6 us (99%)
    pallas_call x1, Pallas kernels, on_device(): pl.pallas_call(functools.partial(kernel, devices), out_shape=[keep((width...  30.8 us
    pallas_call x1, Pallas kernels, on_device(): pl.pallas_call(store, out_shape=jax.ShapeDtypeStruct((tokens, width), BF1...  1.83 us

profile of v4, /device:TPU:25, one launch (start us, length us, event | category | flops | bytes accessed | tf_op | source)
XLA Modules:
  0.0 32.6 jit_solution(14629712712572524295)
XLA Ops:
  0.0 30.8 %layer.1 = (bf16[48,256,128]{2,1,0:T(8,128)(2,1)S(1)}, f32[256,6144]{1,0:T(8,128)S(1)}, bf16[48,256,128]{2,1,0:T(8,128)(2,1)S(1)}, bf16[12,2,256,256]{3,2,1,0:T(8,128)(2,1)S(1)}, f32[1,6144]{1,0:T(1,128)S(1)}) custom-call(bf16[256,6144]{1,0:T(8,128)(2,1)} %q_hbm.1, bf16[256,6144]{1,0:T(8,128)(2,1)} %k_hbm.1, bf16[256,6144]{1,0:T(8,128)(2,1)} %v_hbm.1, ...), custom_call_target="tpu_custom_call" | custom-call | tf_op jit(solution)/shard_map/layer/pallas_call | solution.py:546
  30.8 1.8 %store.1 = bf16[256,6144]{1,0:T(8,128)(2,1)} custom-call(bf16[48,256,128]{2,1,0:T(8,128)(2,1)S(1)} %get-tuple-element.10.done, f32[256,6144]{1,0:T(8,128)S(1)} %get-tuple-element.11.mixed, bf16[48,256,128]{2,1,0:T(8,128)(2,1)S(1)} %get-tuple-element.12.q_feat, bf16[12,2,256,256]{3,2,1,0:T(8,128)(2,1)S(1)} %get-tuple-element.13.prefix, ...), custom_call_target="tpu_custom_call" | custom-call | tf_op jit(solution)/shard_map/store/pallas_call | solution.py:601

commit v5 on v4

--- a/solution.py
+++ b/solution.py
@@ -21,8 +21,8 @@
 CATCH_ONE = 2
 CATCH_TWO = 5
 CATCH_PLANE = 3
-MIX_LAG = 11
-LAST_MIX_LAG = 9
+MIX_LAG = 12
+LAST_MIX_LAG = 10
 TAIL = 2
 
 
@@ -35,12 +35,17 @@
         tall = wide.at[j]
         tap_rows = taps[which, :, lanes].astype(F32)
         tall[RIM - HALO : RIM] = halo[which, :, lanes].astype(F32)
-        rows = buf[:, lanes].astype(F32)
-        tall[RIM:] = rows
-        total = tap_rows[0:1] * rows
-        for offset in range(1, tap_count):
-            total = total + tap_rows[offset : offset + 1] * tall[RIM - offset : RIM - offset + length]
-        out.append(total.astype(BF16))
+        parts = []
+        for top in range(0, length, length // 2):
+            size = length // 2
+            rows = buf[top : top + size, lanes].astype(F32)
+            tall[RIM + top : RIM + top + size] = rows
+            total = tap_rows[0:1] * rows
+            for offset in range(1, tap_count):
+                start = RIM + top - offset
+                total = total + tap_rows[offset : offset + 1] * tall[start : start + size]
+            parts.append(total.astype(BF16))
+        out.append(jnp.concatenate(parts, axis=0))
     return jnp.concatenate(out, axis=1)
 
 

time: 32.8 us -> 32.5 us (level)
  no operation moved by 1% of the time
where the time goes in v5:
time: 32.5 us; the launch traced here: 32.3 us
  Pallas kernels  32.3 us (99%)
    pallas_call x1, Pallas kernels, on_device(): pl.pallas_call(functools.partial(kernel, devices), out_shape=[keep((width...  30.5 us
    pallas_call x1, Pallas kernels, on_device(): pl.pallas_call(store, out_shape=jax.ShapeDtypeStruct((tokens, width), BF1...  1.83 us

profile of v5, /device:TPU:25, one launch (start us, length us, event | category | flops | bytes accessed | tf_op | source)
XLA Modules:
  0.0 32.3 jit_solution(5952785495520584358)
XLA Ops:
  0.0 30.5 %layer.1 = (bf16[48,256,128]{2,1,0:T(8,128)(2,1)S(1)}, f32[256,6144]{1,0:T(8,128)S(1)}, bf16[48,256,128]{2,1,0:T(8,128)(2,1)S(1)}, bf16[12,2,256,256]{3,2,1,0:T(8,128)(2,1)S(1)}, f32[1,6144]{1,0:T(1,128)S(1)}) custom-call(bf16[256,6144]{1,0:T(8,128)(2,1)} %q_hbm.1, bf16[256,6144]{1,0:T(8,128)(2,1)} %k_hbm.1, bf16[256,6144]{1,0:T(8,128)(2,1)} %v_hbm.1, ...), custom_call_target="tpu_custom_call" | custom-call | tf_op jit(solution)/shard_map/layer/pallas_call | solution.py:551
  30.5 1.8 %store.1 = bf16[256,6144]{1,0:T(8,128)(2,1)} custom-call(bf16[48,256,128]{2,1,0:T(8,128)(2,1)S(1)} %get-tuple-element.10.done, f32[256,6144]{1,0:T(8,128)S(1)} %get-tuple-element.11.mixed, bf16[48,256,128]{2,1,0:T(8,128)(2,1)S(1)} %get-tuple-element.12.q_feat, bf16[12,2,256,256]{3,2,1,0:T(8,128)(2,1)S(1)} %get-tuple-element.13.prefix, ...), custom_call_target="tpu_custom_call" | custom-call | tf_op jit(solution)/shard_map/store/pallas_call | solution.py:606

commit v6 on v5

--- a/solution.py
+++ b/solution.py
@@ -18,8 +18,8 @@
 Z_LAG = 3
 R_LAG = 5
 P_LAG = 3
-CATCH_ONE = 2
-CATCH_TWO = 5
+CATCH_ONE = 3
+CATCH_TWO = 6
 CATCH_PLANE = 3
 MIX_LAG = 12
 LAST_MIX_LAG = 10

time: 32.5 us -> 32.4 us (level)
  no operation moved by 1% of the time
where the time goes in v6:
time: 32.4 us; the launch traced here: 32.3 us
  Pallas kernels  32.3 us (100%)
    pallas_call x1, Pallas kernels, on_device(): pl.pallas_call(functools.partial(kernel, devices), out_shape=[keep((width...  30.4 us
    pallas_call x1, Pallas kernels, on_device(): pl.pallas_call(store, out_shape=jax.ShapeDtypeStruct((tokens, width), BF1...  1.83 us

profile of v6, /device:TPU:25, one launch (start us, length us, event | category | flops | bytes accessed | tf_op | source)
XLA Modules:
  0.0 32.3 jit_solution(11092588286841047471)
XLA Ops:
  0.0 30.4 %layer.1 = (bf16[48,256,128]{2,1,0:T(8,128)(2,1)S(1)}, f32[256,6144]{1,0:T(8,128)S(1)}, bf16[48,256,128]{2,1,0:T(8,128)(2,1)S(1)}, bf16[12,2,256,256]{3,2,1,0:T(8,128)(2,1)S(1)}, f32[1,6144]{1,0:T(1,128)S(1)}) custom-call(bf16[256,6144]{1,0:T(8,128)(2,1)} %q_hbm.1, bf16[256,6144]{1,0:T(8,128)(2,1)} %k_hbm.1, bf16[256,6144]{1,0:T(8,128)(2,1)} %v_hbm.1, ...), custom_call_target="tpu_custom_call" | custom-call | tf_op jit(solution)/shard_map/layer/pallas_call | solution.py:551
  30.4 1.8 %store.1 = bf16[256,6144]{1,0:T(8,128)(2,1)} custom-call(bf16[48,256,128]{2,1,0:T(8,128)(2,1)S(1)} %get-tuple-element.10.done, f32[256,6144]{1,0:T(8,128)S(1)} %get-tuple-element.11.mixed, bf16[48,256,128]{2,1,0:T(8,128)(2,1)S(1)} %get-tuple-element.12.q_feat, bf16[12,2,256,256]{3,2,1,0:T(8,128)(2,1)S(1)} %get-tuple-element.13.prefix, ...), custom_call_target="tpu_custom_call" | custom-call | tf_op jit(solution)/shard_map/store/pallas_call | solution.py:606
